TPU v7x, 32 devices: a whole 2x2x4 slice. The times are simulated.
32 devices in a mesh: old: 4 (over y, core), new: 8 (over z, x).
Axes of the slice: x: 2, y: 2, z: 4, core: 2. Of those that a mesh axis runs over, the one named last changes fastest.
Arguments:
- old_field: bfloat16 [3, 27, 98304], P(None, None, ('old', 'new')), may hold values from -6 to 6
- pair_dest: int32 [32768, 1], P(('old', 'new')), may hold values from 0 to 31; in each aligned block of 1024 rows (0 to 1023, 1024 to 2047, ...) at most 128 rows name the same one
- pair_new: int32 [32768], P(('old', 'new')), may hold values from 0 to 511
- pair_old: int32 [32768], P(('old', 'new')), may hold values from 0 to 3071
- pair_block: int32 [32768], P(('old', 'new')), may hold values from 0 to 3
- basis_old: bfloat16 [4, 27, 125], replicated, may hold values from -1.25 to 1.25
- basis_new: bfloat16 [4, 27, 125], replicated, may hold values from -0.5 to 0.5
- volume: float32 [2, 8, 1024], P(None, 'old', 'new'), may hold values from 0.25 to 36, as said below
Outputs:
- solution: float32 [3, 5, 16, 2048], P(None, None, 'old', 'new')
- residual: float32 [3, 5, 16, 2048], P(None, None, 'old', 'new')
Inputs may be any that keep to these rules, and one draw needn't show every extreme that they name: `pair_dest`: a device's index is its position along old times the number of devices along new plus its position along new; in each device's block of 1024 pairs at most 128 name one destination. `pair_new`: local element number (x * 2 + y) * 128 + z within the destination's block. `pair_old`: old element within the block of the device that holds the pair. `volume`: positive element factors.
All inputs are finite; a program needn't handle non-finite values.
Results may differ from a plain program's by a relative error of at most 0.003.
Values may be sent and summed in bfloat16 or wider, within the bound.
A program may use at most 64 MiB of HBM per device.

v0:
```python
import jax
import jax.numpy as jnp
import numpy as np
from jax import lax
from jax.sharding import PartitionSpec as P

ITERS = 4
LINE_MASS = np.array([[4.0, 2.0, -1.0], [2.0, 16.0, 2.0], [-1.0, 2.0, 4.0]]) / 15.0


def passed_along(shard, axis, by):
    size = lax.axis_size(axis)
    return lax.ppermute(shard, axis, [(i, (i + by) % size) for i in range(size)])


def split_axis(array, axis, count):
    moved = jnp.moveaxis(array, axis, -1)
    paired = moved[..., : 2 * count].reshape(moved.shape[:-1] + (count, 2))
    even_nodes = paired[..., 0]
    odd_nodes = paired[..., 1]
    after_nodes = jnp.concatenate(
        [even_nodes[..., 1:], moved[..., 2 * count : 2 * count + 1]], axis=-1
    )
    stacked = jnp.stack([even_nodes, odd_nodes, after_nodes], axis=0)
    return jnp.moveaxis(stacked, -1, axis + 1)


def pick_nodes(extended, cell_counts):
    along_first, along_second, along_third = cell_counts
    stacked = split_axis(extended, 3, along_third)
    stacked = split_axis(stacked, 3, along_second)
    stacked = split_axis(stacked, 3, along_first)
    return jnp.transpose(stacked, (3, 0, 1, 2, 4, 5, 6))


def merge_axis(array, local_axis, cell_axis):
    moved = jnp.moveaxis(array, (local_axis, cell_axis), (0, -1))
    count = moved.shape[-1]
    zero_pad = [(0, 0)] * (moved.ndim - 2)
    even_full = jnp.pad(moved[0], zero_pad + [(0, 1)]) + jnp.pad(moved[2], zero_pad + [(1, 0)])
    woven = jnp.stack([even_full[..., :count], moved[1]], axis=-1)
    woven = woven.reshape(woven.shape[:-2] + (2 * count,))
    return jnp.concatenate([woven, even_full[..., count:]], axis=-1)


def spread_nodes(element_nodes):
    summed = merge_axis(element_nodes, 3, 6)
    summed = merge_axis(summed, 2, 4)
    summed = merge_axis(summed, 1, 2)
    return jnp.transpose(summed, (0, 3, 2, 1))


def element_mass(element_nodes, volume):
    line_mass = jnp.asarray(LINE_MASS, dtype=jnp.float32)
    high = lax.Precision.HIGHEST
    applied = jnp.einsum("ia,cabdxyz->cibdxyz", line_mass, element_nodes, precision=high)
    applied = jnp.einsum("jb,cibdxyz->cijdxyz", line_mass, applied, precision=high)
    applied = jnp.einsum("kd,cijdxyz->cijkxyz", line_mass, applied, precision=high)
    return applied * volume


def fold_rims(assembled):
    front_face = passed_along(assembled[..., -1], "new", 1)
    inner_part = assembled[..., :-1]
    inner_part = jnp.concatenate(
        [inner_part[..., :1] + front_face[..., None], inner_part[..., 1:]], axis=3
    )
    side_face = passed_along(inner_part[:, :, -1, :], "old", 1)
    folded = inner_part[:, :, :-1]
    folded = jnp.concatenate(
        [folded[:, :, :1] + side_face[:, :, None, :], folded[:, :, 1:]], axis=2
    )
    return folded


def operate(vector, volume):
    upper_layer = passed_along(vector[..., 0], "new", -1)
    extended = jnp.concatenate([vector, upper_layer[..., None]], axis=3)
    upper_row = passed_along(extended[:, :, 0, :], "old", -1)
    extended = jnp.concatenate([extended, upper_row[:, :, None, :]], axis=2)
    element_nodes = pick_nodes(extended, volume.shape)
    return fold_rims(spread_nodes(element_mass(element_nodes, volume)))


def quadrature(coefficients, block_kind, basis_old, basis_new):
    summed = jnp.zeros(coefficients.shape, jnp.float32)
    for q in range(basis_old.shape[0]):
        chosen = jnp.where(
            (block_kind == q)[None, None, :], coefficients, jnp.zeros((), coefficients.dtype)
        )
        values = jnp.einsum(
            "cap,ak->ckp", chosen, basis_old[q], preferred_element_type=jnp.float32
        ).astype(jnp.bfloat16)
        summed = summed + jnp.einsum(
            "ckp,ak->cap", values, basis_new[q], preferred_element_type=jnp.float32
        )
    return summed


def squares(residual):
    return lax.psum(jnp.sum(residual * residual, axis=(1, 2, 3)), ("old", "new"))


def on_device(old_field, pair_dest, pair_new, pair_old, pair_block, basis_old, basis_new, volume):
    devices = lax.axis_size(("old", "new"))
    pair_count = pair_dest.shape[0]
    capacity = 4 * pair_count // devices
    cells_one, cells_two, cells_three = volume.shape
    elements = cells_one * cells_two * cells_three
    destination = pair_dest[:, 0]
    onehot = (destination[:, None] == jnp.arange(devices, dtype=jnp.int32)[None, :]).astype(
        jnp.int32
    )
    slot_rank = jnp.sum((jnp.cumsum(onehot, axis=0) - onehot) * onehot, axis=1)
    position = destination * capacity + slot_rank
    gathered = jnp.take(old_field, pair_old, axis=2)
    contribution = quadrature(gathered, pair_block, basis_old, basis_new)
    outgoing = (
        jnp.zeros((81, devices * capacity), jnp.float32)
        .at[:, position]
        .set(contribution.reshape(81, -1))
    )
    targets = jnp.full((devices * capacity,), elements, jnp.int32).at[position].set(pair_new)
    received, slot_element = (
        lax.all_to_all(
            outgoing.reshape(81, devices, capacity),
            ("old", "new"),
            split_axis=1,
            concat_axis=1,
            tiled=True,
        ),
        lax.all_to_all(
            targets.reshape(1, devices, capacity),
            ("old", "new"),
            split_axis=1,
            concat_axis=1,
            tiled=True,
        ),
    )
    arrived = received.reshape(81, -1)
    slot_element = slot_element.reshape(-1)
    element_load = (
        jnp.zeros((81, elements + 1), jnp.float32).at[:, slot_element].add(arrived)[:, :elements]
    )
    load_vector = fold_rims(
        spread_nodes(element_load.reshape(3, 3, 3, 3, cells_one, cells_two, cells_three))
    )
    solution = jnp.zeros_like(load_vector)
    residual = load_vector
    direction = load_vector
    norm_now = squares(residual)
    for iteration in range(ITERS):
        applied = operate(direction, volume)
        curvature = lax.psum(jnp.sum(direction * applied, axis=(1, 2, 3)), ("old", "new"))
        step_size = norm_now / curvature
        solution = solution + step_size[:, None, None, None] * direction
        residual = residual - step_size[:, None, None, None] * applied
        norm_next = squares(residual)
        direction = residual + (norm_next / norm_now)[:, None, None, None] * direction
        norm_now = norm_next
    return (solution, residual)


def solution(mesh):
    in_specs = (
        P(None, None, ("old", "new")),
        P(("old", "new"), None),
        P(("old", "new")),
        P(("old", "new")),
        P(("old", "new")),
        P(),
        P(),
        P(None, "old", "new"),
    )
    out_specs = (P(None, None, "old", "new"), P(None, None, "old", "new"))
    return jax.shard_map(
        on_device, mesh=mesh, in_specs=in_specs, out_specs=out_specs, check_vma=False
    )
```

profile of v0, /device:TPU:10, one launch (start us, length us, event | category | flops | bytes accessed | tf_op | source)
XLA Modules:
  0.0 578.3 jit_solution(5909297454449030575)
XLA Ops:
  1.3 9.0 %reduce-window.6 = s32[32,8,128]{2,1,0:T(8,128)S(1)} reduce-window(s32[32,8,128]{2,1,0:T(8,128)S(1)} %fusion.60, s32[]{:T(128)} %constant.17.clone.1), window={size=1x1x128 pad=0_0x0_0x127_0}, to_apply=%region_0.0 | reduce-window | flops 4161536 | bytes 262148 | tf_op jit(solution)/shard_map/reduce-window
  10.8 0.7 fusion.59
  12.3 5.1 scatter_custom_fusion
  17.3 6.0 %all-to-all-start = ((s32[1,32,128]{2,0,1:T(1,128)}), s32[1,32,128]{2,0,1:T(1,128)S(1)}, u32[]{:S(2)}, u32[]{:S(2)}) async-start(s32[1,32,128]{2,0,1:T(1,128)} %bitcast.6), calls=%async_computation | async-start | bytes 32768 | tf_op jit(solution)/shard_map/all_to_all | solution.py:132
  24.0 0.7 broadcast_compare_fusion.3
  24.8 4.5 copy.623
  30.0 7.5 %gather_fusion = bf16[1024,3,27]{2,1,0:T(4,128)(2,1)} fusion(bf16[3,27,3072]{1,0,2:T(4,128)(2,1)S(1)} %copy.623, s32[1024]{0:T(1024)S(1)} %fusion.106), kind=kCustom, calls=%fused_computation | custom fusion | bytes 335872 | tf_op jit(solution)/shard_map/jit(_take)/gather | solution.py:116
  37.6 9.2 %select_bitcast_fusion.3 = (bf16[3,27,1024]{1,0,2:T(4,128)(2,1)}, bf16[3,27,1024]{1,0,2:T(4,128)(2,1)S(1)}, bf16[3,27,1024]{1,0,2:T(4,128)(2,1)S(1)}, bf16[3,27,1024]{1,0,2:T(4,128)(2,1)S(1)}) fusion(pred[1024]{0:T(1024)(128)(4,1)S(1)} %get-tuple-element.120, bf16[1024,3,27]{2,1,0:T(4,128)(2,1)} %gather_fusion, pred[1024]{0:T(1024)(128)(4,1)S(1)} %get-tuple-element.126, ...), kind=kLoop, calls=%fused_computation.31 | loop fusion | flops 414720 | bytes 834560 | tf_op jit(solution)/shard_map/jit(_where)/select_n | solution.py:88
  46.8 1.4 fusion.6
  48.2 2.3 fusion.5
  50.4 1.4 fusion.4
  51.8 1.7 fusion.11
  53.8 3.8 scatter_custom_fusion.1
  57.6 1.8 copy.641
  59.3 5.8 %all-to-all-start.1 = ((f32[81,32,128]{2,0,1:T(8,128)}), f32[81,32,128]{2,0,1:T(8,128)S(1)}, u32[]{:S(2)}, u32[]{:S(2)}) async-start(f32[81,32,128]{2,0,1:T(8,128)} %copy.641), calls=%async_computation.1 | async-start | bytes 2883584 | tf_op jit(solution)/shard_map/all_to_all | solution.py:125
  65.8 31.4 %all-to-all-done.1 = f32[81,32,128]{2,0,1:T(8,128)S(1)} async-done(((f32[81,32,128]{2,0,1:T(8,128)}), f32[81,32,128]{2,0,1:T(8,128)S(1)}, u32[]{:S(2)}, u32[]{:S(2)}) %all-to-all-start.1) | async-done | bytes 1327136 | tf_op jit(solution)/shard_map/all_to_all | solution.py:125
  97.6 1.0 copy.830
  98.6 0.8 copy.643
  99.4 28.0 %scatter_custom_fusion.2 = f32[81,513]{0,1:T(8,128)S(1)} fusion(s32[4096]{0:T(1024)} %bitcast.616, f32[4096,81]{1,0:T(8,128)S(1)} %copy.643, f32[]{:T(128)} %constant.14.clone.1), kind=kCustom, calls=%fused_computation.113 | custom fusion | flops 331776 | bytes 166724 | tf_op jit(solution)/shard_map/scatter-add | solution.py:143
  128.1 4.3 copy.777
  132.4 6.2 %reshape.241 = f32[3,3,3,2,2,256]{5,4,3,0,1,2:T(2,128)S(1)} reshape(f32[3,3,3,2,2,128,2]{6,5,4,3,0,1,2:T(8,128)} %copy.777) | data formatting | bytes 221184 | tf_op jit(solution)/shard_map/reshape | solution.py:42
  140.1 3.0 collective-permute-done
  143.7 3.0 collective-permute-done.1
  147.0 2.4 collective-permute-start.2
  149.4 2.1 collective-permute-done.2
  151.8 1.6 collective-permute-done.3
  154.1 2.5 fusion.118
  156.6 2.2 copy.806
  162.4 4.3 copy.779
  166.7 6.2 %reshape.242 = f32[3,3,3,2,2,256]{5,4,3,0,1,2:T(2,128)S(1)} reshape(f32[3,3,3,2,2,128,2]{6,5,4,3,0,1,2:T(8,128)} %copy.779) | data formatting | bytes 221184 | tf_op jit(solution)/shard_map/reshape | solution.py:42
  174.5 3.0 collective-permute-done.4
  178.1 2.9 collective-permute-done.5
  181.4 45.8 %all-reduce.30 = (f32[3]{0:T(128)S(1)}, f32[3]{0:T(128)S(1)}) all-reduce(f32[3]{0:T(128)S(1)} %get-tuple-element.7, f32[3]{0:T(128)S(1)} %get-tuple-element.6), channel_id=1, replica_groups=mesh['old'=4,'new'=8] {'old','new'}, use_global_device_ids=true, to_apply=%region_7.8 | all-reduce | flops 6 | bytes 48 | tf_op jit(solution)/shard_map/psum | solution.py:101
  227.4 38.4 %psum.58 = f32[3]{0:T(128)S(1)} all-reduce(f32[3]{0:T(128)S(1)} %get-tuple-element.20), channel_id=1, replica_groups=mesh['old'=4,'new'=8] {'old','new'}, use_global_device_ids=true, to_apply=%region_11.12 | all-reduce | flops 3 | bytes 24 | tf_op jit(solution)/shard_map/psum | solution.py:101
  266.2 4.5 collective-permute-done.6
  271.2 1.6 collective-permute-done.7
  273.4 2.5 fusion.117
  275.9 2.2 copy.812
  281.7 4.3 copy.781
  286.0 6.2 %reshape.243 = f32[3,3,3,2,2,256]{5,4,3,0,1,2:T(2,128)S(1)} reshape(f32[3,3,3,2,2,128,2]{6,5,4,3,0,1,2:T(8,128)} %copy.781) | data formatting | bytes 221184 | tf_op jit(solution)/shard_map/reshape | solution.py:42
  293.2 3.6 collective-permute-done.8
  297.5 2.8 collective-permute-done.9
  300.6 42.8 %psum.59 = f32[3]{0:T(128)S(1)} all-reduce(f32[3]{0:T(128)S(1)} %get-tuple-element.18), channel_id=1, replica_groups=mesh['old'=4,'new'=8] {'old','new'}, use_global_device_ids=true, to_apply=%region_13.14 | all-reduce | flops 3 | bytes 24 | tf_op jit(solution)/shard_map/psum | solution.py:154
  343.6 39.3 %psum.60 = f32[3]{0:T(128)S(1)} all-reduce(f32[3]{0:T(128)S(1)} %get-tuple-element.16), channel_id=1, replica_groups=mesh['old'=4,'new'=8] {'old','new'}, use_global_device_ids=true, to_apply=%region_15.16 | all-reduce | flops 3 | bytes 24 | tf_op jit(solution)/shard_map/psum | solution.py:101
  383.2 4.5 collective-permute-done.10
  388.4 1.6 collective-permute-done.11
  390.7 2.5 fusion.116
  393.1 2.2 copy.818
  399.0 4.3 copy.783
  403.3 6.2 %reshape.244 = f32[3,3,3,2,2,256]{5,4,3,0,1,2:T(2,128)S(1)} reshape(f32[3,3,3,2,2,128,2]{6,5,4,3,0,1,2:T(8,128)} %copy.783) | data formatting | bytes 221184 | tf_op jit(solution)/shard_map/reshape | solution.py:42
  410.4 3.6 collective-permute-done.12
  414.4 3.2 collective-permute-done.13
  417.9 42.8 %psum.61 = f32[3]{0:T(128)S(1)} all-reduce(f32[3]{0:T(128)S(1)} %get-tuple-element.14), channel_id=1, replica_groups=mesh['old'=4,'new'=8] {'old','new'}, use_global_device_ids=true, to_apply=%region_17.18 | all-reduce | flops 3 | bytes 24 | tf_op jit(solution)/shard_map/psum | solution.py:154
  460.9 38.9 %psum.62 = f32[3]{0:T(128)S(1)} all-reduce(f32[3]{0:T(128)S(1)} %get-tuple-element.12), channel_id=1, replica_groups=mesh['old'=4,'new'=8] {'old','new'}, use_global_device_ids=true, to_apply=%region_19.20 | all-reduce | flops 3 | bytes 24 | tf_op jit(solution)/shard_map/psum | solution.py:101
  500.1 4.5 collective-permute-done.14
  505.0 1.6 collective-permute-done.15
  507.3 2.5 fusion.115
  509.8 2.2 copy.824
  515.6 4.3 copy.785
  519.9 6.2 %reshape.245 = f32[3,3,3,2,2,256]{5,4,3,0,1,2:T(2,128)S(1)} reshape(f32[3,3,3,2,2,128,2]{6,5,4,3,0,1,2:T(8,128)} %copy.785) | data formatting | bytes 221184 | tf_op jit(solution)/shard_map/reshape | solution.py:42
  527.1 3.6 collective-permute-done.16
  531.1 3.1 collective-permute-done.17
  534.5 42.8 %psum.63 = f32[3]{0:T(128)S(1)} all-reduce(f32[3]{0:T(128)S(1)} %get-tuple-element.10), channel_id=1, replica_groups=mesh['old'=4,'new'=8] {'old','new'}, use_global_device_ids=true, to_apply=%region_21.22 | all-reduce | flops 3 | bytes 24 | tf_op jit(solution)/shard_map/psum | solution.py:154
  577.3 0.8 multiply_subtract_fusion
  (333 shorter events, 34.3 us)
Async XLA Ops:
  10.8 18.5 %copy-start.2 = (bf16[4,27,125]{2,0,1:T(4,128)(2,1)S(1)}, bf16[4,27,125]{2,0,1:T(4,128)(2,1)}, u32[]{:S(2)}) copy-start(bf16[4,27,125]{2,0,1:T(4,128)(2,1)} %param.17) | copy-start | bytes 81004
  10.8 18.5 %copy-start.3 = (bf16[4,27,125]{2,0,1:T(4,128)(2,1)S(1)}, bf16[4,27,125]{2,0,1:T(4,128)(2,1)}, u32[]{:S(2)}) copy-start(bf16[4,27,125]{2,0,1:T(4,128)(2,1)} %param.18) | copy-start | bytes 81004
  12.3 11.8 %copy-start.5 = (s32[1024,1]{0,1:T(1,128)}, s32[1024,1]{0,1:T(1,128)S(1)}, u32[]{:S(2)}) copy-start(s32[1024,1]{0,1:T(1,128)S(1)} %compare_select_fusion.1) | copy-start | bytes 12292
  17.3 42.0 %all-to-all-start = ((s32[1,32,128]{2,0,1:T(1,128)}), s32[1,32,128]{2,0,1:T(1,128)S(1)}, u32[]{:S(2)}, u32[]{:S(2)}) async-start(s32[1,32,128]{2,0,1:T(1,128)} %bitcast.6), calls=%async_computation | async-start | bytes 32768 | tf_op jit(solution)/shard_map/all_to_all | solution.py:132
  48.2 3.6 copy-start
  59.3 37.9 %all-to-all-start.1 = ((f32[81,32,128]{2,0,1:T(8,128)}), f32[81,32,128]{2,0,1:T(8,128)S(1)}, u32[]{:S(2)}, u32[]{:S(2)}) async-start(f32[81,32,128]{2,0,1:T(8,128)} %copy.641), calls=%async_computation.1 | async-start | bytes 2883584 | tf_op jit(solution)/shard_map/all_to_all | solution.py:125
  139.4 3.7 collective-permute-start
  143.4 3.3 collective-permute-start.1
  147.0 4.6 collective-permute-start.2
  151.7 1.6 collective-permute-start.3
  158.8 1.5 copy-start.1
  159.6 2.4 copy-start.4
  173.8 3.7 collective-permute-start.4
  177.8 3.3 collective-permute-start.5
  266.1 4.6 collective-permute-start.6
  270.9 1.8 collective-permute-start.7
  293.1 3.7 collective-permute-start.8
  297.1 3.3 collective-permute-start.9
  383.2 4.6 collective-permute-start.10
  387.9 2.0 collective-permute-start.11
  410.3 3.7 collective-permute-start.12
  414.3 3.3 collective-permute-start.13
  500.0 4.6 collective-permute-start.14
  504.8 1.8 collective-permute-start.15
  526.9 3.7 collective-permute-start.16
  530.9 3.3 collective-permute-start.17
where the time goes:
time: 588 us; the launch traced here: 578 us
  blocking collectives  291 us (49%)
  local copies, waits for them, and re-layouts  109 us (19%)
  waiting for transfers between devices  85.1 us (14%)
  other arithmetic  59.1 us (10%)
  starting transfers between devices  17.8 us (3%)
  matrix products  13.5 us (2%)
    psum x4, blocking collectives, squares(): lax.psum(jnp.sum(residual * residual, axis=(1, 2, 3)), ('old', 'new'))  162 us
    psum x3, blocking collectives, on_device(): lax.psum(jnp.sum(direction * applied, axis=(1, 2, 3)), ('old', 'new'))  128 us
    ppermute x18, waiting for transfers between devices, passed_along(): lax.ppermute(shard, axis, [(i, (i + by) % size) for i in range(size)])  53.7 us
    reshape x20, local copies, waits for them, and re-layouts, merge_axis(): woven = woven.reshape(woven.shape[:-2] + (2 * count,))  52.6 us
    all_to_all x1, waiting for transfers between devices, on_device(): lax.all_to_all(outgoing.reshape(81, devices, capacity), ('old', 'new'), s...  31.4 us
    scatter-add x1, other arithmetic, on_device(): jnp.zeros((81, elements + 1), jnp.float32).at[:, slot_element].add(arrived)  28 us
    unnamed x39, local copies, waits for them, and re-layouts  16.9 us
  transfers between devices with their start and end apart: 20, of which 19 were waited for; matrix products, arithmetic and copies ran while one was open for 6% of the time, Pallas kernels for 0%

commit v1 on v0

--- a/solution.py
+++ b/solution.py
@@ -1,11 +1,21 @@
+import functools
 import jax
 import jax.numpy as jnp
 import numpy as np
 from jax import lax
 from jax.sharding import PartitionSpec as P
+from jax.lax import psum
 
 ITERS = 4
 LINE_MASS = np.array([[4.0, 2.0, -1.0], [2.0, 16.0, 2.0], [-1.0, 2.0, 4.0]]) / 15.0
+
+
+def marks_launch(field_in, mesh_dim, axis_tag):
+    r1 = psum(field_in, mesh_dim)
+    return psum(r1, axis_tag)
+
+
+pair_edge_on = functools.partial(marks_launch, mesh_dim="old", axis_tag="new")
 
 
 def passed_along(shard, axis, by):
@@ -151,7 +161,7 @@
     norm_now = squares(residual)
     for iteration in range(ITERS):
         applied = operate(direction, volume)
-        curvature = lax.psum(jnp.sum(direction * applied, axis=(1, 2, 3)), ("old", "new"))
+        curvature = pair_edge_on(jnp.sum(direction * applied, axis=(1, 2, 3)))
         step_size = norm_now / curvature
         solution = solution + step_size[:, None, None, None] * direction
         residual = residual - step_size[:, None, None, None] * applied

time: 588 us -> 566 us (0.963)
  the two profiles are of different devices: /device:TPU:10 before, /device:TPU:0 now
where the time goes in v1:
time: 566 us; the launch traced here: 557 us
  blocking collectives  250 us (44%)
  local copies, waits for them, and re-layouts  109 us (19%)
  waiting for transfers between devices  90.3 us (16%)
  other arithmetic  57.9 us (10%)
  starting transfers between devices  32.9 us (6%)
  matrix products  13.5 us (2%)
    psum x4, blocking collectives, squares(): lax.psum(jnp.sum(residual * residual, axis=(1, 2, 3)), ('old', 'new'))  153 us
    psum x4, blocking collectives, marks_launch(): return psum(r1, axis_tag)  74.1 us
    ppermute x18, waiting for transfers between devices, passed_along(): lax.ppermute(shard, axis, [(i, (i + by) % size) for i in range(size)])  55 us
    reshape x20, local copies, waits for them, and re-layouts, merge_axis(): woven = woven.reshape(woven.shape[:-2] + (2 * count,))  52.7 us
    all_to_all x1, waiting for transfers between devices, on_device(): lax.all_to_all(outgoing.reshape(81, devices, capacity), ('old', 'new'), s...  35.3 us
    scatter-add x1, other arithmetic, on_device(): jnp.zeros((81, elements + 1), jnp.float32).at[:, slot_element].add(arrived)  26.7 us
    psum x4, blocking collectives, marks_launch(): r1 = psum(field_in, mesh_dim)  22.9 us
    ppermute x18, starting transfers between devices, passed_along(): lax.ppermute(shard, axis, [(i, (i + by) % size) for i in range(size)])  19.8 us
  transfers between devices with their start and end apart: 20, of which 19 were waited for; matrix products, arithmetic and copies ran while one was open for 7% of the time, Pallas kernels for 0%

profile of v1, /device:TPU:0, one launch (start us, length us, event | category | flops | bytes accessed | tf_op | source)
XLA Modules:
  0.0 556.8 jit_solution(1704380572184772029)
XLA Ops:
  1.3 9.0 %reduce-window.6 = s32[32,8,128]{2,1,0:T(8,128)S(1)} reduce-window(s32[32,8,128]{2,1,0:T(8,128)S(1)} %fusion.60, s32[]{:T(128)} %constant.17.clone.1), window={size=1x1x128 pad=0_0x0_0x127_0}, to_apply=%region_0.0 | reduce-window | flops 4161536 | bytes 262148 | tf_op jit(solution)/shard_map/reduce-window
  12.3 5.1 scatter_custom_fusion
  17.3 7.3 %all-to-all-start = ((s32[1,32,128]{2,0,1:T(1,128)}), s32[1,32,128]{2,0,1:T(1,128)S(1)}, u32[]{:S(2)}, u32[]{:S(2)}) async-start(s32[1,32,128]{2,0,1:T(1,128)} %bitcast.6), calls=%async_computation | async-start | bytes 32768 | tf_op jit(solution)/shard_map/all_to_all | solution.py:142
  26.1 4.5 copy.623
  31.3 7.5 %gather_fusion = bf16[1024,3,27]{2,1,0:T(4,128)(2,1)} fusion(bf16[3,27,3072]{1,0,2:T(4,128)(2,1)S(1)} %copy.623, s32[1024]{0:T(1024)S(1)} %fusion.106), kind=kCustom, calls=%fused_computation | custom fusion | bytes 335872 | tf_op jit(solution)/shard_map/jit(_take)/gather | solution.py:126
  38.9 9.2 %select_bitcast_fusion.3 = (bf16[3,27,1024]{1,0,2:T(4,128)(2,1)}, bf16[3,27,1024]{1,0,2:T(4,128)(2,1)S(1)}, bf16[3,27,1024]{1,0,2:T(4,128)(2,1)S(1)}, bf16[3,27,1024]{1,0,2:T(4,128)(2,1)S(1)}) fusion(pred[1024]{0:T(1024)(128)(4,1)S(1)} %get-tuple-element.118, bf16[1024,3,27]{2,1,0:T(4,128)(2,1)} %gather_fusion, pred[1024]{0:T(1024)(128)(4,1)S(1)} %get-tuple-element.124, ...), kind=kLoop, calls=%fused_computation.31 | loop fusion | flops 414720 | bytes 834560 | tf_op jit(solution)/shard_map/jit(_where)/select_n | solution.py:98
  49.5 2.2 fusion.5
  53.1 1.7 fusion.11
  55.1 3.8 scatter_custom_fusion.1
  58.9 1.7 copy.641
  60.6 5.8 %all-to-all-start.1 = ((f32[81,32,128]{2,0,1:T(8,128)}), f32[81,32,128]{2,0,1:T(8,128)S(1)}, u32[]{:S(2)}, u32[]{:S(2)}) async-start(f32[81,32,128]{2,0,1:T(8,128)} %copy.641), calls=%async_computation.1 | async-start | bytes 2883584 | tf_op jit(solution)/shard_map/all_to_all | solution.py:135
  67.1 35.3 %all-to-all-done.1 = f32[81,32,128]{2,0,1:T(8,128)S(1)} async-done(((f32[81,32,128]{2,0,1:T(8,128)}), f32[81,32,128]{2,0,1:T(8,128)S(1)}, u32[]{:S(2)}, u32[]{:S(2)}) %all-to-all-start.1) | async-done | bytes 1327136 | tf_op jit(solution)/shard_map/all_to_all | solution.py:135
  104.6 26.7 %scatter_custom_fusion.2 = f32[81,513]{0,1:T(8,128)S(1)} fusion(s32[4096]{0:T(1024)} %bitcast.616, f32[4096,81]{1,0:T(8,128)S(1)} %copy.643, f32[]{:T(128)} %constant.14.clone.1), kind=kCustom, calls=%fused_computation.113 | custom fusion | flops 331776 | bytes 166724 | tf_op jit(solution)/shard_map/scatter-add | solution.py:153
  132.0 4.3 copy.777
  136.3 6.2 %reshape.241 = f32[3,3,3,2,2,256]{5,4,3,0,1,2:T(2,128)S(1)} reshape(f32[3,3,3,2,2,128,2]{6,5,4,3,0,1,2:T(8,128)} %copy.777) | data formatting | bytes 221184 | tf_op jit(solution)/shard_map/reshape | solution.py:52
  143.3 1.6 collective-permute-start
  145.0 4.7 collective-permute-done
  150.2 3.1 collective-permute-done.1
  153.6 3.6 collective-permute-done.2
  157.5 1.6 collective-permute-done.3
  159.8 2.5 fusion.118
  162.3 2.2 copy.806
  168.2 4.3 copy.779
  172.5 6.2 %reshape.242 = f32[3,3,3,2,2,256]{5,4,3,0,1,2:T(2,128)S(1)} reshape(f32[3,3,3,2,2,128,2]{6,5,4,3,0,1,2:T(8,128)} %copy.779) | data formatting | bytes 221184 | tf_op jit(solution)/shard_map/reshape | solution.py:52
  179.7 6.3 %collective-permute-done.4 = f32[3,5,5]{2,0,1:T(4,128)S(1)} collective-permute-done((f32[3,5,5]{2,0,1:T(4,128)S(1)}, f32[3,5,5]{2,0,1:T(4,128)S(1)}, u32[]{:S(2)}, u32[]{:S(2)}) %collective-permute-start.4) | collective-permute-done | bytes 332 | tf_op jit(solution)/shard_map/ppermute | solution.py:23
  186.3 3.2 collective-permute-done.5
  189.8 5.7 %psum.85 = f32[3]{0:T(128)S(1)} all-reduce(f32[3]{0:T(128)S(1)} %get-tuple-element.6), channel_id=1, replica_groups=mesh['old'=4,'new'=8] {'old'}, use_global_device_ids=true, to_apply=%region_9.10 | all-reduce | flops 3 | bytes 24 | tf_op jit(solution)/shard_map/psum | solution.py:14
  195.5 17.1 %psum.86 = f32[3]{0:T(128)S(1)} all-reduce(f32[3]{0:T(128)S(1)} %psum.85), channel_id=1, replica_groups=mesh['old'=4,'new'=8] {'new'}, use_global_device_ids=true, to_apply=%region_10.11 | all-reduce | flops 3 | bytes 24 | tf_op jit(solution)/shard_map/psum | solution.py:15
  212.6 37.4 %psum.84 = f32[3]{0:T(128)S(1)} all-reduce(f32[3]{0:T(128)S(1)} %get-tuple-element.7), channel_id=1, replica_groups=mesh['old'=4,'new'=8] {'old','new'}, use_global_device_ids=true, to_apply=%region_7.8 | all-reduce | flops 3 | bytes 24 | tf_op jit(solution)/shard_map/psum | solution.py:111
  250.2 42.1 %psum.87 = f32[3]{0:T(128)S(1)} all-reduce(f32[3]{0:T(128)S(1)} %get-tuple-element.18), channel_id=1, replica_groups=mesh['old'=4,'new'=8] {'old','new'}, use_global_device_ids=true, to_apply=%region_12.13 | all-reduce | flops 3 | bytes 24 | tf_op jit(solution)/shard_map/psum | solution.py:111
  292.6 3.3 collective-permute-start.6
  297.8 1.6 collective-permute-done.7
  300.0 2.5 fusion.117
  302.5 2.2 copy.812
  308.3 4.3 copy.781
  312.7 6.2 %reshape.243 = f32[3,3,3,2,2,256]{5,4,3,0,1,2:T(2,128)S(1)} reshape(f32[3,3,3,2,2,128,2]{6,5,4,3,0,1,2:T(8,128)} %copy.781) | data formatting | bytes 221184 | tf_op jit(solution)/shard_map/reshape | solution.py:52
  319.7 2.2 collective-permute-start.8
  322.0 4.3 collective-permute-done.8
  326.8 3.1 collective-permute-done.9
  330.2 5.6 %psum.88 = f32[3]{0:T(128)S(1)} all-reduce(f32[3]{0:T(128)S(1)} %get-tuple-element.16), channel_id=1, replica_groups=mesh['old'=4,'new'=8] {'old'}, use_global_device_ids=true, to_apply=%region_14.15 | all-reduce | flops 3 | bytes 24 | tf_op jit(solution)/shard_map/psum | solution.py:14
  335.9 19.1 %psum.89 = f32[3]{0:T(128)S(1)} all-reduce(f32[3]{0:T(128)S(1)} %psum.88), channel_id=1, replica_groups=mesh['old'=4,'new'=8] {'new'}, use_global_device_ids=true, to_apply=%region_15.16 | all-reduce | flops 3 | bytes 24 | tf_op jit(solution)/shard_map/psum | solution.py:15
  355.2 36.8 %psum.90 = f32[3]{0:T(128)S(1)} all-reduce(f32[3]{0:T(128)S(1)} %get-tuple-element.14), channel_id=1, replica_groups=mesh['old'=4,'new'=8] {'old','new'}, use_global_device_ids=true, to_apply=%region_17.18 | all-reduce | flops 3 | bytes 24 | tf_op jit(solution)/shard_map/psum | solution.py:111
  392.3 4.0 collective-permute-start.10
  398.3 1.6 collective-permute-done.11
  400.6 2.5 fusion.116
  403.0 2.2 copy.818
  408.9 4.3 copy.783
  413.2 6.2 %reshape.244 = f32[3,3,3,2,2,256]{5,4,3,0,1,2:T(2,128)S(1)} reshape(f32[3,3,3,2,2,128,2]{6,5,4,3,0,1,2:T(8,128)} %copy.783) | data formatting | bytes 221184 | tf_op jit(solution)/shard_map/reshape | solution.py:52
  420.2 1.5 collective-permute-start.12
  421.8 5.1 collective-permute-done.12
  427.4 3.1 collective-permute-done.13
  430.8 5.9 %psum.91 = f32[3]{0:T(128)S(1)} all-reduce(f32[3]{0:T(128)S(1)} %get-tuple-element.12), channel_id=1, replica_groups=mesh['old'=4,'new'=8] {'old'}, use_global_device_ids=true, to_apply=%region_19.20 | all-reduce | flops 3 | bytes 24 | tf_op jit(solution)/shard_map/psum | solution.py:14
  436.7 18.8 %psum.92 = f32[3]{0:T(128)S(1)} all-reduce(f32[3]{0:T(128)S(1)} %psum.91), channel_id=1, replica_groups=mesh['old'=4,'new'=8] {'new'}, use_global_device_ids=true, to_apply=%region_20.21 | all-reduce | flops 3 | bytes 24 | tf_op jit(solution)/shard_map/psum | solution.py:15
  455.7 36.8 %psum.93 = f32[3]{0:T(128)S(1)} all-reduce(f32[3]{0:T(128)S(1)} %get-tuple-element.10), channel_id=1, replica_groups=mesh['old'=4,'new'=8] {'old','new'}, use_global_device_ids=true, to_apply=%region_22.23 | all-reduce | flops 3 | bytes 24 | tf_op jit(solution)/shard_map/psum | solution.py:111
  492.8 4.0 collective-permute-start.14
  498.6 1.6 collective-permute-done.15
  500.9 2.5 fusion.115
  503.3 2.2 copy.824
  509.2 4.3 copy.785
  513.5 6.2 %reshape.245 = f32[3,3,3,2,2,256]{5,4,3,0,1,2:T(2,128)S(1)} reshape(f32[3,3,3,2,2,128,2]{6,5,4,3,0,1,2:T(8,128)} %copy.785) | data formatting | bytes 221184 | tf_op jit(solution)/shard_map/reshape | solution.py:52
  522.1 5.1 collective-permute-done.16
  527.7 3.1 collective-permute-done.17
  531.1 5.6 %psum.94 = f32[3]{0:T(128)S(1)} all-reduce(f32[3]{0:T(128)S(1)} %get-tuple-element.8), channel_id=1, replica_groups=mesh['old'=4,'new'=8] {'old'}, use_global_device_ids=true, to_apply=%region_24.25 | all-reduce | flops 3 | bytes 24 | tf_op jit(solution)/shard_map/psum | solution.py:14
  536.7 19.1 %psum.95 = f32[3]{0:T(128)S(1)} all-reduce(f32[3]{0:T(128)S(1)} %psum.94), channel_id=1, replica_groups=mesh['old'=4,'new'=8] {'new'}, use_global_device_ids=true, to_apply=%region_25.26 | all-reduce | flops 3 | bytes 24 | tf_op jit(solution)/shard_map/psum | solution.py:15
  (338 shorter events, 44.8 us)
Async XLA Ops:
  10.8 19.8 %copy-start.2 = (bf16[4,27,125]{2,0,1:T(4,128)(2,1)S(1)}, bf16[4,27,125]{2,0,1:T(4,128)(2,1)}, u32[]{:S(2)}) copy-start(bf16[4,27,125]{2,0,1:T(4,128)(2,1)} %param.17) | copy-start | bytes 81004
  10.8 19.8 %copy-start.3 = (bf16[4,27,125]{2,0,1:T(4,128)(2,1)S(1)}, bf16[4,27,125]{2,0,1:T(4,128)(2,1)}, u32[]{:S(2)}) copy-start(bf16[4,27,125]{2,0,1:T(4,128)(2,1)} %param.18) | copy-start | bytes 81004
  12.3 13.1 %copy-start.5 = (s32[1024,1]{0,1:T(1,128)}, s32[1024,1]{0,1:T(1,128)S(1)}, u32[]{:S(2)}) copy-start(s32[1024,1]{0,1:T(1,128)S(1)} %compare_select_fusion.1) | copy-start | bytes 12292
  17.3 43.3 %all-to-all-start = ((s32[1,32,128]{2,0,1:T(1,128)}), s32[1,32,128]{2,0,1:T(1,128)S(1)}, u32[]{:S(2)}, u32[]{:S(2)}) async-start(s32[1,32,128]{2,0,1:T(1,128)} %bitcast.6), calls=%async_computation | async-start | bytes 32768 | tf_op jit(solution)/shard_map/all_to_all | solution.py:142
  49.5 3.6 copy-start
  60.6 41.7 %all-to-all-start.1 = ((f32[81,32,128]{2,0,1:T(8,128)}), f32[81,32,128]{2,0,1:T(8,128)S(1)}, u32[]{:S(2)}, u32[]{:S(2)}) async-start(f32[81,32,128]{2,0,1:T(8,128)} %copy.641), calls=%async_computation.1 | async-start | bytes 2883584 | tf_op jit(solution)/shard_map/all_to_all | solution.py:135
  143.3 6.4 %collective-permute-start = (f32[3,5,5]{2,0,1:T(4,128)S(1)}, f32[3,5,5]{2,0,1:T(4,128)S(1)}, u32[]{:S(2)}, u32[]{:S(2)}) collective-permute-start(f32[3,5,5]{2,0,1:T(4,128)S(1)} %bitcast.617), channel_id=1, source_target_pairs={{0,1},{1,2},{2,3},{3,4},{4,5},{5,6},{6,7},{7,0},{8,9},{9,10},{10,1... | collective-permute-start | bytes 908 | tf_op jit(solution)/shard_map/ppermute | solution.py:23
  150.0 3.3 collective-permute-start.1
  153.6 3.7 collective-permute-start.2
  157.5 1.6 collective-permute-start.3
  164.5 1.5 copy-start.1
  165.3 2.4 copy-start.4
  179.5 6.4 %collective-permute-start.4 = (f32[3,5,5]{2,0,1:T(4,128)S(1)}, f32[3,5,5]{2,0,1:T(4,128)S(1)}, u32[]{:S(2)}, u32[]{:S(2)}) collective-permute-start(f32[3,5,5]{2,0,1:T(4,128)S(1)} %bitcast.619), channel_id=1, source_target_pairs={{0,1},{1,2},{2,3},{3,4},{4,5},{5,6},{6,7},{7,0},{8,9},{9,10},{10,1... | collective-permute-start | bytes 908 | tf_op jit(solution)/shard_map/ppermute | solution.py:23
  186.3 3.3 collective-permute-start.5
  292.6 4.6 collective-permute-start.6
  297.5 1.8 collective-permute-start.7
  319.7 6.6 %collective-permute-start.8 = (f32[3,5,5]{2,0,1:T(4,128)S(1)}, f32[3,5,5]{2,0,1:T(4,128)S(1)}, u32[]{:S(2)}, u32[]{:S(2)}) collective-permute-start(f32[3,5,5]{2,0,1:T(4,128)S(1)} %bitcast.621), channel_id=1, source_target_pairs={{0,1},{1,2},{2,3},{3,4},{4,5},{5,6},{6,7},{7,0},{8,9},{9,10},{10,1... | collective-permute-start | bytes 908 | tf_op jit(solution)/shard_map/ppermute | solution.py:23
  326.7 3.3 collective-permute-start.9
  392.3 5.4 collective-permute-start.10
  397.8 2.0 collective-permute-start.11
  420.2 6.7 %collective-permute-start.12 = (f32[3,5,5]{2,0,1:T(4,128)S(1)}, f32[3,5,5]{2,0,1:T(4,128)S(1)}, u32[]{:S(2)}, u32[]{:S(2)}) collective-permute-start(f32[3,5,5]{2,0,1:T(4,128)S(1)} %bitcast.623), channel_id=1, source_target_pairs={{0,1},{1,2},{2,3},{3,4},{4,5},{5,6},{6,7},{7,0},{8,9},{9,10},{10,1... | collective-permute-start | bytes 908 | tf_op jit(solution)/shard_map/ppermute | solution.py:23
  427.2 3.3 collective-permute-start.13
  492.8 5.4 collective-permute-start.14
  498.4 1.8 collective-permute-start.15
  520.5 6.7 %collective-permute-start.16 = (f32[3,5,5]{2,0,1:T(4,128)S(1)}, f32[3,5,5]{2,0,1:T(4,128)S(1)}, u32[]{:S(2)}, u32[]{:S(2)}) collective-permute-start(f32[3,5,5]{2,0,1:T(4,128)S(1)} %bitcast.625), channel_id=1, source_target_pairs={{0,1},{1,2},{2,3},{3,4},{4,5},{5,6},{6,7},{7,0},{8,9},{9,10},{10,1... | collective-permute-start | bytes 908 | tf_op jit(solution)/shard_map/ppermute | solution.py:23
  527.5 3.3 collective-permute-start.17
